TPU v7x, 256 devices: a whole 4x4x8 slice. The times are simulated.
256 devices in a mesh: aper: 64 (over z_hi, y, x), shot: 4 (over z_lo, core).
Axes of the slice: x: 4, y: 4, z: 8 (z_hi: 4, z_lo: 2; z = z_hi * 2 + z_lo), core: 2. Of those that a mesh axis runs over, the one named last changes fastest.
Arguments:
- wavefield: float32 [4, 9, 256, 128, 128], P('shot', None, 'aper'), may hold values from -6 to 6
- lame_lambda: float32 [256, 128, 128], P('aper', 'shot'), may hold values from 0.5 to 2
- lame_mu: float32 [256, 128, 128], P('aper', 'shot'), may hold values from 0.3 to 1
- buoyancy: float32 [256, 128, 128], P('aper', 'shot'), may hold values from 0.4 to 1
- quality: float32 [256, 128, 128], P('aper', 'shot'), may hold values from 0.05 to 2
- active: int32 [4, 64, 4, 4], replicated, may hold values 0 or 1
Outputs:
- final_field: float32 [4, 9, 256, 128, 128], P('shot', None, 'aper')
All inputs are finite; a program needn't handle non-finite values.
Results may differ from a plain program's by a relative error of at most 0.00002.
Values sent between devices are 32-bit elements; how exact they have to be, the bound alone decides.
A program may use at most 64 MiB of HBM per device.

v0:
```python
import jax
import jax.numpy as jnp
from jax import lax
from jax.sharding import PartitionSpec as P

BLK = 32
STEPS = 4


COEF_NEAR = 1.125
COEF_FAR = -1.0 / 24.0
TIME_STEP = 0.2


def extended(shard, sides, width):
    for axis, dim in sides:
        devices, length = (lax.axis_size(axis), shard.shape[dim])
        up = [(i, (i + 1) % devices) for i in range(devices - 1)]
        down = [(j, i) for i, j in up]
        last = lax.slice_in_dim(shard, length - width, length, axis=dim)
        initial = lax.slice_in_dim(shard, 0, width, axis=dim)
        before = lax.ppermute(last, axis, up)
        after = lax.ppermute(initial, axis, down)
        shard = jnp.concatenate([before, shard, after], axis=dim)
    return shard


def forward_rows(values, offset, length):
    return COEF_NEAR * (
        values[offset + 1 : offset + 1 + length] - values[offset : offset + length]
    ) + COEF_FAR * (
        values[offset + 2 : offset + 2 + length] - values[offset - 1 : offset - 1 + length]
    )


def backward_rows(values, offset, length):
    return COEF_NEAR * (
        values[offset : offset + length] - values[offset - 1 : offset - 1 + length]
    ) + COEF_FAR * (
        values[offset + 1 : offset + 1 + length] - values[offset - 2 : offset - 2 + length]
    )


def shifted(values, along, amount):
    widths = [(0, 0)] * values.ndim
    widths[along] = (2, 2)
    padded = jnp.pad(values, widths)
    return lax.slice_in_dim(padded, 2 + amount, 2 + amount + values.shape[along], axis=along)


def forward_axis(values, along):
    return COEF_NEAR * (shifted(values, along, 1) - values) + COEF_FAR * (
        shifted(values, along, 2) - shifted(values, along, -1)
    )


def backward_axis(values, along):
    return COEF_NEAR * (values - shifted(values, along, -1)) + COEF_FAR * (
        shifted(values, along, 1) - shifted(values, along, -2)
    )


def velocity_update(previous, stress, offset, length, buoyancy, damping, active_cells):

    def pick_rows(values):
        return values[offset : offset + length]

    grad_first = (
        forward_rows(stress[0], offset, length)
        + backward_axis(pick_rows(stress[3]), 1)
        + backward_axis(pick_rows(stress[4]), 2)
    )
    grad_second = (
        backward_rows(stress[3], offset, length)
        + forward_axis(pick_rows(stress[1]), 1)
        + backward_axis(pick_rows(stress[5]), 2)
    )
    grad_third = (
        backward_rows(stress[4], offset, length)
        + backward_axis(pick_rows(stress[5]), 1)
        + forward_axis(pick_rows(stress[2]), 2)
    )
    forcing = jnp.stack([grad_first, grad_second, grad_third])
    return previous + active_cells * (
        damping * (previous + TIME_STEP * buoyancy * forcing) - previous
    )


def stress_update(previous, velocity, offset, length, lambda_field, shear, damping, active_cells):

    def pick_rows(values):
        return values[offset : offset + length]

    strain_first = backward_rows(velocity[0], offset, length)
    strain_second = backward_axis(pick_rows(velocity[1]), 1)
    strain_third = backward_axis(pick_rows(velocity[2]), 2)
    dilation = strain_first + strain_second + strain_third
    shear_xy = forward_axis(pick_rows(velocity[0]), 1) + forward_rows(velocity[1], offset, length)
    shear_xz = forward_axis(pick_rows(velocity[0]), 2) + forward_rows(velocity[2], offset, length)
    shear_yz = forward_axis(pick_rows(velocity[1]), 2) + forward_axis(pick_rows(velocity[2]), 1)
    rates = jnp.stack(
        [
            lambda_field * dilation + 2.0 * shear * strain_first,
            lambda_field * dilation + 2.0 * shear * strain_second,
            lambda_field * dilation + 2.0 * shear * strain_third,
            shear * shear_xy,
            shear * shear_xz,
            shear * shear_yz,
        ]
    )
    return previous + active_cells * (damping * (previous + TIME_STEP * rates) - previous)


def upsample(blocks):
    return jnp.repeat(jnp.repeat(blocks, BLK, axis=1), BLK, axis=2)


def per_device(wavefield, lame_lambda, lame_mu, buoyancy, quality, active):
    panels = (
        lax.all_gather(lame_lambda, "shot", axis=1, tiled=True),
        lax.all_gather(lame_mu, "shot", axis=1, tiled=True),
        lax.all_gather(buoyancy, "shot", axis=1, tiled=True),
        lax.all_gather(quality, "shot", axis=1, tiled=True),
    )
    model = jnp.stack(panels)
    values = wavefield[0]
    slab_rows = values.shape[1]
    device = lax.axis_index("aper")
    damping = jnp.exp(-TIME_STEP * model[3])
    for moment in range(STEPS):
        blocks = lax.dynamic_index_in_dim(
            active[moment].astype(jnp.float32), device, 0, keepdims=True
        )
        active_cells = upsample(blocks)
        stress_pad = extended(values[3:], (("aper", 1),), 2)
        velocity = velocity_update(
            values[:3], stress_pad, 2, slab_rows, model[2], damping, active_cells
        )
        velocity_pad = extended(velocity, (("aper", 1),), 2)
        stress = stress_update(
            values[3:], velocity_pad, 2, slab_rows, model[0], model[1], damping, active_cells
        )
        values = jnp.concatenate([velocity, stress], axis=0)
    return values[None]


def solution(mesh):
    return jax.shard_map(
        per_device,
        mesh=mesh,
        in_specs=(
            P("shot", None, "aper", None, None),
            P("aper", "shot", None),
            P("aper", "shot", None),
            P("aper", "shot", None),
            P("aper", "shot", None),
            P(),
        ),
        out_specs=P("shot", None, "aper", None, None),
        check_vma=False,
    )
```

profile of v0, /device:TPU:126, one launch (start us, length us, event | category | flops | bytes accessed | tf_op | source)
XLA Modules:
  0.0 352.6 jit_solution(15949601193661434074)
XLA Ops:
  0.0 1.5 slice_bitcast_fusion
  1.5 1.2 fusion.436
  2.8 2.7 collective-permute-start
  5.5 9.4 %collective-permute-start.1 = (f32[6,2,128,128]{3,2,1,0:T(8,128)}, f32[6,2,128,128]{3,2,1,0:T(8,128)}, u32[]{:S(2)}, u32[]{:S(2)}) collective-permute-start(f32[6,2,128,128]{3,2,1,0:T(8,128)} %get-tuple-element.48), channel_id=1, source_target_pairs={{0,4},{4,8},{8,12},{12,16},{16,20},{20,24},{24,28},{28,32},{32,36}... | collective-permute-start | bytes 2359304 | tf_op jit(solution)/shard_map/ppermute | solution.py:22
  15.0 0.6 fusion.441
  15.6 35.7 %all_gather.12 = f32[4,128,128]{2,1,0:T(8,128)S(1)} all-gather(f32[4,32,128]{2,1,0:T(8,128)S(1)} %copy-done.41), channel_id=1, replica_groups=mesh['aper'=64,'shot'=4] {'shot'}, dimensions={1}, use_global_device_ids=true | all-gather | bytes 327680 | tf_op jit(solution)/shard_map/all_gather | solution.py:123
  51.4 5.8 %all_gather.13 = f32[4,128,128]{2,1,0:T(8,128)S(1)} all-gather(f32[4,32,128]{2,1,0:T(8,128)S(1)} %copy-done.42), channel_id=1, replica_groups=mesh['aper'=64,'shot'=4] {'shot'}, dimensions={1}, use_global_device_ids=true | all-gather | bytes 327680 | tf_op jit(solution)/shard_map/all_gather | solution.py:122
  57.7 1.6 slice_bitcast_fusion.32
  59.3 0.6 copy-done
  59.9 1.3 fusion.31
  61.2 1.3 fusion.38
  62.5 1.2 fusion.24
  64.0 0.4 copy-done.15
  64.4 1.9 collective-permute-start.2
  66.3 3.9 %collective-permute-start.3 = (f32[3,2,128,128]{3,2,1,0:T(8,128)S(1)}, f32[3,2,128,128]{3,2,1,0:T(8,128)S(1)}, u32[]{:S(2)}, u32[]{:S(2)}) collective-permute-start(f32[3,2,128,128]{3,2,1,0:T(8,128)S(1)} %get-tuple-element.68), channel_id=1, source_target_pairs={{4,0},{8,4},{12,8},{16,12},{20,16},{24,20},{28,24},{32,28},{36,32}... | collective-permute-start | bytes 1179656 | tf_op jit(solution)/shard_map/ppermute | solution.py:23
  70.3 15.9 %all_gather.15 = f32[4,128,128]{2,1,0:T(8,128)S(1)} all-gather(f32[4,32,128]{2,1,0:T(8,128)S(1)} %copy-done.43), channel_id=1, replica_groups=mesh['aper'=64,'shot'=4] {'shot'}, dimensions={1}, use_global_device_ids=true | all-gather | bytes 327680 | tf_op jit(solution)/shard_map/all_gather | solution.py:121
  86.2 5.8 %all_gather.14 = f32[4,128,128]{2,1,0:T(8,128)S(1)} all-gather(f32[4,32,128]{2,1,0:T(8,128)S(1)} %copy-done.44), channel_id=1, replica_groups=mesh['aper'=64,'shot'=4] {'shot'}, dimensions={1}, use_global_device_ids=true | all-gather | bytes 327680 | tf_op jit(solution)/shard_map/all_gather | solution.py:120
  92.4 0.4 copy-done.19
  94.0 1.2 fusion.435
  95.2 1.9 collective-permute-start.4
  97.1 12.7 %collective-permute-start.5 = (f32[6,2,128,128]{3,2,1,0:T(8,128)}, f32[6,2,128,128]{3,2,1,0:T(8,128)}, u32[]{:S(2)}, u32[]{:S(2)}) collective-permute-start(f32[6,2,128,128]{3,2,1,0:T(8,128)} %get-tuple-element.46), channel_id=1, source_target_pairs={{0,4},{4,8},{8,12},{12,16},{16,20},{20,24},{24,28},{28,32},{32,36}... | collective-permute-start | bytes 2359304 | tf_op jit(solution)/shard_map/ppermute | solution.py:22
  110.1 0.6 broadcast_in_dim.61
  110.8 0.9 copy.10
  111.8 30.2 %collective-permute-done.4 = f32[6,2,128,128]{3,2,1,0:T(8,128)S(1)} collective-permute-done((f32[6,2,128,128]{3,2,1,0:T(8,128)}, f32[6,2,128,128]{3,2,1,0:T(8,128)S(1)}, u32[]{:S(2)}, u32[]{:S(2)}) %collective-permute-start.4) | collective-permute-done | bytes 786464 | tf_op jit(solution)/shard_map/ppermute | solution.py:23
  142.0 2.3 collective-permute-done.5
  144.4 1.3 fusion.75
  145.6 1.3 fusion.82
  147.0 1.2 fusion.68
  148.3 1.6 fusion.9
  150.0 10.7 %collective-permute-start.6 = (f32[3,2,128,128]{3,2,1,0:T(8,128)S(1)}, f32[3,2,128,128]{3,2,1,0:T(8,128)S(1)}, u32[]{:S(2)}, u32[]{:S(2)}) collective-permute-start(f32[3,2,128,128]{3,2,1,0:T(8,128)S(1)} %get-tuple-element.62), channel_id=1, source_target_pairs={{0,4},{4,8},{8,12},{12,16},{16,20},{20,24},{24,28},{28,32},{32,36}... | collective-permute-start | bytes 1179656 | tf_op jit(solution)/shard_map/ppermute | solution.py:22
  160.7 1.9 collective-permute-start.7
  162.7 10.9 %collective-permute-done.6 = f32[3,2,128,128]{3,2,1,0:T(8,128)S(1)} collective-permute-done((f32[3,2,128,128]{3,2,1,0:T(8,128)S(1)}, f32[3,2,128,128]{3,2,1,0:T(8,128)S(1)}, u32[]{:S(2)}, u32[]{:S(2)}) %collective-permute-start.6) | collective-permute-done | bytes 393248 | tf_op jit(solution)/shard_map/ppermute | solution.py:22
  173.5 9.0 %collective-permute-done.7 = f32[3,2,128,128]{3,2,1,0:T(8,128)S(1)} collective-permute-done((f32[3,2,128,128]{3,2,1,0:T(8,128)S(1)}, f32[3,2,128,128]{3,2,1,0:T(8,128)S(1)}, u32[]{:S(2)}, u32[]{:S(2)}) %collective-permute-start.7) | collective-permute-done | bytes 393248 | tf_op jit(solution)/shard_map/ppermute | solution.py:23
  183.6 0.4 copy-done.2
  184.4 1.3 fusion.434
  185.7 1.9 collective-permute-start.8
  187.6 10.2 %collective-permute-start.9 = (f32[6,2,128,128]{3,2,1,0:T(8,128)}, f32[6,2,128,128]{3,2,1,0:T(8,128)S(1)}, u32[]{:S(2)}, u32[]{:S(2)}) collective-permute-start(f32[6,2,128,128]{3,2,1,0:T(8,128)} %get-tuple-element.39), channel_id=1, source_target_pairs={{0,4},{4,8},{8,12},{12,16},{16,20},{20,24},{24,28},{28,32},{32,36}... | collective-permute-start | bytes 2359304 | tf_op jit(solution)/shard_map/ppermute | solution.py:22
  197.9 0.7 copy.21
  198.6 0.8 broadcast_in_dim.63
  199.4 0.7 broadcast_in_dim.64
  200.0 1.3 broadcast_in_dim.65
  201.3 1.6 copy.13
  203.0 25.6 %collective-permute-done.8 = f32[6,2,128,128]{3,2,1,0:T(8,128)S(1)} collective-permute-done((f32[6,2,128,128]{3,2,1,0:T(8,128)}, f32[6,2,128,128]{3,2,1,0:T(8,128)S(1)}, u32[]{:S(2)}, u32[]{:S(2)}) %collective-permute-start.8) | collective-permute-done | bytes 786464 | tf_op jit(solution)/shard_map/ppermute | solution.py:23
  228.6 1.3 collective-permute-done.9
  232.1 1.7 fusion.14
  233.9 10.7 %collective-permute-start.10 = (f32[3,2,128,128]{3,2,1,0:T(8,128)S(1)}, f32[3,2,128,128]{3,2,1,0:T(8,128)S(1)}, u32[]{:S(2)}, u32[]{:S(2)}) collective-permute-start(f32[3,2,128,128]{3,2,1,0:T(8,128)S(1)} %get-tuple-element.57), channel_id=1, source_target_pairs={{0,4},{4,8},{8,12},{12,16},{16,20},{20,24},{24,28},{28,32},{32,36}... | collective-permute-start | bytes 1179656 | tf_op jit(solution)/shard_map/ppermute | solution.py:22
  244.6 2.1 collective-permute-start.11
  246.8 8.4 %collective-permute-done.10 = f32[3,2,128,128]{3,2,1,0:T(8,128)S(1)} collective-permute-done((f32[3,2,128,128]{3,2,1,0:T(8,128)S(1)}, f32[3,2,128,128]{3,2,1,0:T(8,128)S(1)}, u32[]{:S(2)}, u32[]{:S(2)}) %collective-permute-start.10) | collective-permute-done | bytes 393248 | tf_op jit(solution)/shard_map/ppermute | solution.py:22
  255.2 16.0 %collective-permute-done.11 = f32[3,2,128,128]{3,2,1,0:T(8,128)S(1)} collective-permute-done((f32[3,2,128,128]{3,2,1,0:T(8,128)S(1)}, f32[3,2,128,128]{3,2,1,0:T(8,128)S(1)}, u32[]{:S(2)}, u32[]{:S(2)}) %collective-permute-start.11) | collective-permute-done | bytes 393248 | tf_op jit(solution)/shard_map/ppermute | solution.py:23
  272.7 1.3 fusion.433
  274.0 1.9 collective-permute-start.12
  275.9 10.2 %collective-permute-start.13 = (f32[6,2,128,128]{3,2,1,0:T(8,128)}, f32[6,2,128,128]{3,2,1,0:T(8,128)S(1)}, u32[]{:S(2)}, u32[]{:S(2)}) collective-permute-start(f32[6,2,128,128]{3,2,1,0:T(8,128)} %get-tuple-element.32), channel_id=1, source_target_pairs={{0,4},{4,8},{8,12},{12,16},{16,20},{20,24},{24,28},{28,32},{32,36}... | collective-permute-start | bytes 2359304 | tf_op jit(solution)/shard_map/ppermute | solution.py:22
  286.2 0.7 copy.22
  286.9 0.7 broadcast_in_dim.67
  287.7 0.6 broadcast_in_dim.69
  288.3 1.6 copy.16
  290.0 25.6 %collective-permute-done.12 = f32[6,2,128,128]{3,2,1,0:T(8,128)S(1)} collective-permute-done((f32[6,2,128,128]{3,2,1,0:T(8,128)}, f32[6,2,128,128]{3,2,1,0:T(8,128)S(1)}, u32[]{:S(2)}, u32[]{:S(2)}) %collective-permute-start.12) | collective-permute-done | bytes 786464 | tf_op jit(solution)/shard_map/ppermute | solution.py:23
  316.8 0.5 copy-done.4
  318.1 1.8 fusion.19
  320.0 10.6 %collective-permute-start.14 = (f32[3,2,128,128]{3,2,1,0:T(8,128)S(1)}, f32[3,2,128,128]{3,2,1,0:T(8,128)S(1)}, u32[]{:S(2)}, u32[]{:S(2)}) collective-permute-start(f32[3,2,128,128]{3,2,1,0:T(8,128)S(1)} %get-tuple-element.52), channel_id=1, source_target_pairs={{0,4},{4,8},{8,12},{12,16},{16,20},{20,24},{24,28},{28,32},{32,36}... | collective-permute-start | bytes 1179656 | tf_op jit(solution)/shard_map/ppermute | solution.py:22
  330.6 1.9 collective-permute-start.15
  332.6 6.5 %collective-permute-done.14 = f32[3,2,128,128]{3,2,1,0:T(8,128)S(1)} collective-permute-done((f32[3,2,128,128]{3,2,1,0:T(8,128)S(1)}, f32[3,2,128,128]{3,2,1,0:T(8,128)S(1)}, u32[]{:S(2)}, u32[]{:S(2)}) %collective-permute-start.14) | collective-permute-done | bytes 393248 | tf_op jit(solution)/shard_map/ppermute | solution.py:22
  339.1 10.4 %collective-permute-done.15 = f32[3,2,128,128]{3,2,1,0:T(8,128)S(1)} collective-permute-done((f32[3,2,128,128]{3,2,1,0:T(8,128)S(1)}, f32[3,2,128,128]{3,2,1,0:T(8,128)S(1)}, u32[]{:S(2)}, u32[]{:S(2)}) %collective-permute-start.15) | collective-permute-done | bytes 393248 | tf_op jit(solution)/shard_map/ppermute | solution.py:23
  351.0 1.6 maximum_bitcast_fusion
  (155 shorter events, 11.7 us)
Async XLA Ops:
  1.5 13.5 %copy-start.45 = (s32[4,64,4,4]{1,3,2,0:T(4,128)S(1)}, s32[4,64,4,4]{1,3,2,0:T(4,128)}, u32[]{:S(2)}) copy-start(s32[4,64,4,4]{1,3,2,0:T(4,128)} %param.11) | copy-start | bytes 49156
  1.5 14.1 %copy-start.41 = (f32[4,32,128]{2,1,0:T(8,128)S(1)}, f32[4,32,128]{2,1,0:T(8,128)}, u32[]{:S(2)}) copy-start(f32[4,32,128]{2,1,0:T(8,128)} %param.10) | copy-start | bytes 196612
  1.5 49.8 %copy-start.42 = (f32[4,32,128]{2,1,0:T(8,128)S(1)}, f32[4,32,128]{2,1,0:T(8,128)}, u32[]{:S(2)}) copy-start(f32[4,32,128]{2,1,0:T(8,128)} %param.9) | copy-start | bytes 196612
  2.8 56.5 %collective-permute-start = (f32[6,2,128,128]{3,2,1,0:T(8,128)}, f32[6,2,128,128]{3,2,1,0:T(8,128)S(1)}, u32[]{:S(2)}, u32[]{:S(2)}) collective-permute-start(f32[6,2,128,128]{3,2,1,0:T(8,128)} %get-tuple-element.47), channel_id=1, source_target_pairs={{4,0},{8,4},{12,8},{16,12},{20,16},{24,20},{28,24},{32,28},{36,32}... | collective-permute-start | bytes 2359304 | tf_op jit(solution)/shard_map/ppermute | solution.py:23
  5.5 53.8 %collective-permute-start.1 = (f32[6,2,128,128]{3,2,1,0:T(8,128)}, f32[6,2,128,128]{3,2,1,0:T(8,128)}, u32[]{:S(2)}, u32[]{:S(2)}) collective-permute-start(f32[6,2,128,128]{3,2,1,0:T(8,128)} %get-tuple-element.48), channel_id=1, source_target_pairs={{0,4},{4,8},{8,12},{12,16},{16,20},{20,24},{24,28},{28,32},{32,36}... | collective-permute-start | bytes 2359304 | tf_op jit(solution)/shard_map/ppermute | solution.py:22
  57.6 90.6 %copy-start.1 = (f32[4,128,128]{2,1,0:T(8,128)}, f32[4,128,128]{2,1,0:T(8,128)S(1)}, u32[]{:S(2)}) copy-start(f32[4,128,128]{2,1,0:T(8,128)S(1)} %multiply_exponential_fusion) | copy-start | bytes 786436
  57.6 2.2 copy-start
  57.7 90.5 %copy-start.5 = (f32[4,128,128]{2,1,0:T(8,128)}, f32[4,128,128]{2,1,0:T(8,128)S(1)}, u32[]{:S(2)}) copy-start(f32[4,128,128]{2,1,0:T(8,128)S(1)} %broadcast_multiply_fusion.1) | copy-start | bytes 786436
  61.2 87.1 %copy-start.8 = (f32[1,4,128,128]{3,2,1,0:T(8,128)}, f32[1,4,128,128]{3,2,1,0:T(8,128)S(1)}, u32[]{:S(2)}) copy-start(f32[1,4,128,128]{3,2,1,0:T(8,128)S(1)} %fusion.31) | copy-start | bytes 786436
  62.5 1.2 copy-start.11
  63.7 0.7 copy-start.15
  63.7 6.5 %copy-start.43 = (f32[4,32,128]{2,1,0:T(8,128)S(1)}, f32[4,32,128]{2,1,0:T(8,128)}, u32[]{:S(2)}) copy-start(f32[4,32,128]{2,1,0:T(8,128)} %param.8) | copy-start | bytes 196612
  63.9 22.3 %copy-start.44 = (f32[4,32,128]{2,1,0:T(8,128)S(1)}, f32[4,32,128]{2,1,0:T(8,128)}, u32[]{:S(2)}) copy-start(f32[4,32,128]{2,1,0:T(8,128)} %param.7) | copy-start | bytes 196612
  64.4 27.7 %collective-permute-start.2 = (f32[3,2,128,128]{3,2,1,0:T(8,128)S(1)}, f32[3,2,128,128]{3,2,1,0:T(8,128)S(1)}, u32[]{:S(2)}, u32[]{:S(2)}) collective-permute-start(f32[3,2,128,128]{3,2,1,0:T(8,128)S(1)} %get-tuple-element.67), channel_id=1, source_target_pairs={{0,4},{4,8},{8,12},{12,16},{16,20},{20,24},{24,28},{28,32},{32,36}... | collective-permute-start | bytes 1179656 | tf_op jit(solution)/shard_map/ppermute | solution.py:22
  66.3 25.8 %collective-permute-start.3 = (f32[3,2,128,128]{3,2,1,0:T(8,128)S(1)}, f32[3,2,128,128]{3,2,1,0:T(8,128)S(1)}, u32[]{:S(2)}, u32[]{:S(2)}) collective-permute-start(f32[3,2,128,128]{3,2,1,0:T(8,128)S(1)} %get-tuple-element.68), channel_id=1, source_target_pairs={{4,0},{8,4},{12,8},{16,12},{20,16},{24,20},{28,24},{32,28},{36,32}... | collective-permute-start | bytes 1179656 | tf_op jit(solution)/shard_map/ppermute | solution.py:23
  92.1 0.7 copy-start.19
  95.2 46.8 %collective-permute-start.4 = (f32[6,2,128,128]{3,2,1,0:T(8,128)}, f32[6,2,128,128]{3,2,1,0:T(8,128)S(1)}, u32[]{:S(2)}, u32[]{:S(2)}) collective-permute-start(f32[6,2,128,128]{3,2,1,0:T(8,128)} %get-tuple-element.45), channel_id=1, source_target_pairs={{4,0},{8,4},{12,8},{16,12},{20,16},{24,20},{28,24},{32,28},{36,32}... | collective-permute-start | bytes 2359304 | tf_op jit(solution)/shard_map/ppermute | solution.py:23
  97.1 47.2 %collective-permute-start.5 = (f32[6,2,128,128]{3,2,1,0:T(8,128)}, f32[6,2,128,128]{3,2,1,0:T(8,128)}, u32[]{:S(2)}, u32[]{:S(2)}) collective-permute-start(f32[6,2,128,128]{3,2,1,0:T(8,128)} %get-tuple-element.46), channel_id=1, source_target_pairs={{0,4},{4,8},{8,12},{12,16},{16,20},{20,24},{24,28},{28,32},{32,36}... | collective-permute-start | bytes 2359304 | tf_op jit(solution)/shard_map/ppermute | solution.py:22
  145.6 2.6 copy-start.23
  147.0 1.3 copy-start.26
  147.0 1.3 copy-start.12
  147.0 1.3 copy-start.16
  148.3 1.6 copy-start.29
  149.9 32.6 %copy-start.20 = (f32[4,128,128]{2,1,0:T(8,128)S(1)}, f32[4,128,128]{2,1,0:T(8,128)}, u32[]{:S(2)}) copy-start(f32[4,128,128]{2,1,0:T(8,128)} %copy-done.19) | copy-start | bytes 786436
  150.0 23.6 %collective-permute-start.6 = (f32[3,2,128,128]{3,2,1,0:T(8,128)S(1)}, f32[3,2,128,128]{3,2,1,0:T(8,128)S(1)}, u32[]{:S(2)}, u32[]{:S(2)}) collective-permute-start(f32[3,2,128,128]{3,2,1,0:T(8,128)S(1)} %get-tuple-element.62), channel_id=1, source_target_pairs={{0,4},{4,8},{8,12},{12,16},{16,20},{20,24},{24,28},{28,32},{32,36}... | collective-permute-start | bytes 1179656 | tf_op jit(solution)/shard_map/ppermute | solution.py:22
  160.7 21.8 %collective-permute-start.7 = (f32[3,2,128,128]{3,2,1,0:T(8,128)S(1)}, f32[3,2,128,128]{3,2,1,0:T(8,128)S(1)}, u32[]{:S(2)}, u32[]{:S(2)}) collective-permute-start(f32[3,2,128,128]{3,2,1,0:T(8,128)S(1)} %get-tuple-element.63), channel_id=1, source_target_pairs={{4,0},{8,4},{12,8},{16,12},{20,16},{24,20},{28,24},{32,28},{36,32}... | collective-permute-start | bytes 1179656 | tf_op jit(solution)/shard_map/ppermute | solution.py:23
  183.1 1.0 copy-start.2
  184.4 13.5 %copy-start.46 = (s32[1,64,4,4]{1,3,2,0:T(4,128)S(1)}, s32[1,64,4,4]{1,3,2,0:T(4,128)}, u32[]{:S(2)}) copy-start(s32[1,64,4,4]{1,3,2,0:T(4,128)} %get-tuple-element.69) | copy-start | bytes 12292
  184.4 13.5 %copy-start.47 = (s32[1,64,4,4]{1,3,2,0:T(4,128)S(1)}, s32[1,64,4,4]{1,3,2,0:T(4,128)}, u32[]{:S(2)}) copy-start(s32[1,64,4,4]{1,3,2,0:T(4,128)} %get-tuple-element.72) | copy-start | bytes 12292
  185.7 43.0 %collective-permute-start.8 = (f32[6,2,128,128]{3,2,1,0:T(8,128)}, f32[6,2,128,128]{3,2,1,0:T(8,128)S(1)}, u32[]{:S(2)}, u32[]{:S(2)}) collective-permute-start(f32[6,2,128,128]{3,2,1,0:T(8,128)} %get-tuple-element.38), channel_id=1, source_target_pairs={{4,0},{8,4},{12,8},{16,12},{20,16},{24,20},{28,24},{32,28},{36,32}... | collective-permute-start | bytes 2359304 | tf_op jit(solution)/shard_map/ppermute | solution.py:23
  187.6 42.3 %collective-permute-start.9 = (f32[6,2,128,128]{3,2,1,0:T(8,128)}, f32[6,2,128,128]{3,2,1,0:T(8,128)S(1)}, u32[]{:S(2)}, u32[]{:S(2)}) collective-permute-start(f32[6,2,128,128]{3,2,1,0:T(8,128)} %get-tuple-element.39), channel_id=1, source_target_pairs={{0,4},{4,8},{8,12},{12,16},{16,20},{20,24},{24,28},{28,32},{32,36}... | collective-permute-start | bytes 2359304 | tf_op jit(solution)/shard_map/ppermute | solution.py:22
  230.2 0.7 copy-start.32
  230.5 0.7 copy-start.34
  230.5 1.0 copy-start.3
  230.5 1.1 copy-start.6
  230.5 1.2 copy-start.9
  230.6 1.3 copy-start.13
  230.6 1.3 copy-start.17
  230.6 1.4 copy-start.24
  230.6 1.5 copy-start.27
  230.6 1.5 copy-start.30
  230.6 1.5 copy-start.38
  232.1 1.7 copy-start.36
  233.8 37.4 %copy-start.21 = (f32[4,128,128]{2,1,0:T(8,128)S(1)}, f32[4,128,128]{2,1,0:T(8,128)}, u32[]{:S(2)}) copy-start(f32[4,128,128]{2,1,0:T(8,128)} %copy-done.19) | copy-start | bytes 786436
  233.9 21.3 %collective-permute-start.10 = (f32[3,2,128,128]{3,2,1,0:T(8,128)S(1)}, f32[3,2,128,128]{3,2,1,0:T(8,128)S(1)}, u32[]{:S(2)}, u32[]{:S(2)}) collective-permute-start(f32[3,2,128,128]{3,2,1,0:T(8,128)S(1)} %get-tuple-element.57), channel_id=1, source_target_pairs={{0,4},{4,8},{8,12},{12,16},{16,20},{20,24},{24,28},{28,32},{32,36}... | collective-permute-start | bytes 1179656 | tf_op jit(solution)/shard_map/ppermute | solution.py:22
  244.6 26.6 %collective-permute-start.11 = (f32[3,2,128,128]{3,2,1,0:T(8,128)S(1)}, f32[3,2,128,128]{3,2,1,0:T(8,128)S(1)}, u32[]{:S(2)}, u32[]{:S(2)}) collective-permute-start(f32[3,2,128,128]{3,2,1,0:T(8,128)S(1)} %get-tuple-element.58), channel_id=1, source_target_pairs={{4,0},{8,4},{12,8},{16,12},{20,16},{24,20},{28,24},{32,28},{36,32}... | collective-permute-start | bytes 1179656 | tf_op jit(solution)/shard_map/ppermute | solution.py:23
  274.0 41.6 %collective-permute-start.12 = (f32[6,2,128,128]{3,2,1,0:T(8,128)}, f32[6,2,128,128]{3,2,1,0:T(8,128)S(1)}, u32[]{:S(2)}, u32[]{:S(2)}) collective-permute-start(f32[6,2,128,128]{3,2,1,0:T(8,128)} %get-tuple-element.31), channel_id=1, source_target_pairs={{4,0},{8,4},{12,8},{16,12},{20,16},{24,20},{28,24},{32,28},{36,32}... | collective-permute-start | bytes 2359304 | tf_op jit(solution)/shard_map/ppermute | solution.py:23
  275.9 39.9 %collective-permute-start.13 = (f32[6,2,128,128]{3,2,1,0:T(8,128)}, f32[6,2,128,128]{3,2,1,0:T(8,128)S(1)}, u32[]{:S(2)}, u32[]{:S(2)}) collective-permute-start(f32[6,2,128,128]{3,2,1,0:T(8,128)} %get-tuple-element.32), channel_id=1, source_target_pairs={{0,4},{4,8},{8,12},{12,16},{16,20},{20,24},{24,28},{28,32},{32,36}... | collective-permute-start | bytes 2359304 | tf_op jit(solution)/shard_map/ppermute | solution.py:22
  316.4 1.0 copy-start.4
  316.4 1.0 copy-start.7
  316.4 1.1 copy-start.10
  316.4 1.2 copy-start.14
  316.4 1.2 copy-start.18
  316.4 1.3 copy-start.25
  316.4 1.4 copy-start.28
  316.4 1.4 copy-start.31
  316.4 1.5 copy-start.33
  316.4 1.6 copy-start.35
  316.5 1.7 copy-start.37
  316.5 1.7 copy-start.39
  316.5 1.6 copy-start.40
  319.9 29.7 %copy-start.22 = (f32[4,128,128]{2,1,0:T(8,128)S(1)}, f32[4,128,128]{2,1,0:T(8,128)}, u32[]{:S(2)}) copy-start(f32[4,128,128]{2,1,0:T(8,128)} %copy-done.19) | copy-start | bytes 786436
  320.0 19.2 %collective-permute-start.14 = (f32[3,2,128,128]{3,2,1,0:T(8,128)S(1)}, f32[3,2,128,128]{3,2,1,0:T(8,128)S(1)}, u32[]{:S(2)}, u32[]{:S(2)}) collective-permute-start(f32[3,2,128,128]{3,2,1,0:T(8,128)S(1)} %get-tuple-element.52), channel_id=1, source_target_pairs={{0,4},{4,8},{8,12},{12,16},{16,20},{20,24},{24,28},{28,32},{32,36}... | collective-permute-start | bytes 1179656 | tf_op jit(solution)/shard_map/ppermute | solution.py:22
  330.6 19.0 %collective-permute-start.15 = (f32[3,2,128,128]{3,2,1,0:T(8,128)S(1)}, f32[3,2,128,128]{3,2,1,0:T(8,128)S(1)}, u32[]{:S(2)}, u32[]{:S(2)}) collective-permute-start(f32[3,2,128,128]{3,2,1,0:T(8,128)S(1)} %get-tuple-element.53), channel_id=1, source_target_pairs={{4,0},{8,4},{12,8},{16,12},{20,16},{24,20},{28,24},{32,28},{36,32}... | collective-permute-start | bytes 1179656 | tf_op jit(solution)/shard_map/ppermute | solution.py:23
where the time goes:
time: 354 us; the launch traced here: 353 us
  waiting for transfers between devices  146 us (41%)
  starting transfers between devices  94.9 us (27%)
  blocking collectives  63.3 us (18%)
  local copies, waits for them, and re-layouts  24.8 us (7%)
  other arithmetic  22.2 us (6%)
    ppermute x8, waiting for transfers between devices, extended(): after = lax.ppermute(initial, axis, down)  117 us
    ppermute x8, starting transfers between devices, extended(): before = lax.ppermute(last, axis, up)  76.6 us
    all_gather x1, blocking collectives, per_device(): lax.all_gather(quality, 'shot', axis=1, tiled=True)  35.7 us
    ppermute x8, waiting for transfers between devices, extended(): before = lax.ppermute(last, axis, up)  29.6 us
    ppermute x8, starting transfers between devices, extended(): after = lax.ppermute(initial, axis, down)  18.3 us
    all_gather x1, blocking collectives, per_device(): lax.all_gather(lame_mu, 'shot', axis=1, tiled=True)  15.9 us
    another operation x12, other arithmetic, velocity_update(): forcing = jnp.stack([grad_first, grad_second, grad_third])  9.36 us
    broadcast_in_dim x16, local copies, waits for them, and re-layouts, upsample(): return jnp.repeat(jnp.repeat(blocks, BLK, axis=1), BLK, axis=2)  9.27 us
  transfers between devices with their start and end apart: 16, of which 12 were waited for; matrix products, arithmetic and copies ran while one was open for 4% of the time, Pallas kernels for 0%

commit v1 on v0

v1 whole, which is shorter than its diff:
```python
import functools

import jax
import jax.numpy as jnp
from jax import lax
from jax.experimental import pallas as pl
from jax.experimental.pallas import tpu as pltpu
from jax.sharding import PartitionSpec as P

BLK = 32
STEPS = 4
TIME_STEP = 0.2
MESH = pl.DeviceIdType.MESH

VX, VY, VZ, SXX, SYY, SZZ, SXY, SXZ, SYZ = range(9)
LAM, MU, BUO, QUA = range(4)
ROWS = 4
NY = 128
NZ = 128
PAD = 8
LO = 2

LAYERS = {SXX: (1, 2), SXY: (2, 1), SXZ: (2, 1), VX: (2, 1), VY: (1, 2), VZ: (1, 2)}


def kernel(n_aper, n_shot, w, lam, mu, buo, qua, act, out, fields, model, masks, blocks, load_sem, act_sem, own_sem,
           gather_send, gather_recv, halo_send, halo_recv, out_sem):
    me = lax.axis_index("aper")
    shot = lax.axis_index("shot")
    has_up = me < n_aper - 1
    has_down = me > 0
    up = jnp.minimum(me + 1, n_aper - 1)
    down = jnp.maximum(me - 1, 0)
    width = NY // n_shot
    mine = pl.ds(pl.multiple_of(shot * width, width), width)
    shards = (lam, mu, buo, qua)

    def inside(f, rows):
        return fields.at[f, rows, PAD:PAD + NY, :]

    def halo(f, to_up, source=None):
        count = LAYERS[f][0 if to_up else 1]
        if to_up:
            rows, there = (LO + ROWS - count, LO - count)
        else:
            rows, there = (LO, LO + ROWS)
        if source is None:
            src = inside(f, pl.ds(rows, count))
        else:
            src = source.at[f, pl.ds(rows - LO, count)]
        side = 0 if to_up else 1
        return pltpu.make_async_remote_copy(
            src_ref=src, dst_ref=inside(f, pl.ds(there, count)), send_sem=halo_send.at[f, side],
            recv_sem=halo_recv.at[f, side], device_id=(up if to_up else down, shot), device_id_type=MESH)

    def send(f, source=None):
        @pl.when(has_up)
        def _():
            halo(f, True, source).start()

        @pl.when(has_down)
        def _():
            halo(f, False, source).start()

    def sent(f):
        @pl.when(has_up)
        def _():
            halo(f, True).wait_send()

        @pl.when(has_down)
        def _():
            halo(f, False).wait_send()

    def arrived(f):
        @pl.when(has_down)
        def _():
            halo(f, True).wait_recv()

        @pl.when(has_up)
        def _():
            halo(f, False).wait_recv()

    def share(f, step):
        peer = lax.rem(shot + step, n_shot)
        return pltpu.make_async_remote_copy(
            src_ref=shards[f], dst_ref=model.at[f, :, mine, :], send_sem=gather_send.at[f, step - 1],
            recv_sem=gather_recv.at[f, step - 1], device_id=(me, peer), device_id_type=MESH)

    loads = [pltpu.make_async_copy(w.at[f], inside(f, pl.ds(LO, ROWS)), load_sem.at[f]) for f in range(9)]
    own = [pltpu.make_async_copy(shards[f], model.at[f, :, mine, :], own_sem.at[f]) for f in range(4)]
    flags = pltpu.make_async_copy(act, blocks, act_sem)

    barrier = pltpu.get_barrier_semaphore()

    @pl.when(has_up)
    def _():
        pl.semaphore_signal(barrier, inc=1, device_id=(up, shot), device_id_type=MESH)

    @pl.when(has_down)
    def _():
        pl.semaphore_signal(barrier, inc=1, device_id=(down, shot), device_id_type=MESH)

    for step in range(1, n_shot):
        pl.semaphore_signal(barrier, inc=1, device_id=(me, lax.rem(shot + step, n_shot)), device_id_type=MESH)

    flags.start()
    for copy in loads + own:
        copy.start()

    zeros = jnp.zeros((ROWS, PAD, NZ), jnp.float32)
    for f in range(9):
        fields[f, LO:LO + ROWS, 0:PAD, :] = zeros
        fields[f, LO:LO + ROWS, PAD + NY:, :] = zeros

    @pl.when(jnp.logical_not(has_down))
    def _():
        for f in LAYERS:
            fields[f, 0:LO, PAD:PAD + NY, :] = jnp.zeros((LO, NY, NZ), jnp.float32)

    @pl.when(jnp.logical_not(has_up))
    def _():
        for f in LAYERS:
            fields[f, LO + ROWS:, PAD:PAD + NY, :] = jnp.zeros((LO, NY, NZ), jnp.float32)

    pl.semaphore_wait(barrier, n_shot - 1 + has_up.astype(jnp.int32) + has_down.astype(jnp.int32))

    for f in (SXX, SXY, SXZ):
        send(f, w)
    for f in (QUA, BUO, LAM, MU):
        for step in range(1, n_shot):
            share(f, step).start()

    lane = lax.broadcasted_iota(jnp.int32, (8, NZ), 1)
    flags.wait()
    for t in range(STEPS):
        for b in range(NY // BLK):
            on = [blocks[t, b, k, me].astype(jnp.float32) for k in range(NZ // BLK)]
            masks[t, b] = jnp.where(lane < BLK, on[0], jnp.where(lane < 2 * BLK, on[1],
                                    jnp.where(lane < 3 * BLK, on[2], on[3])))

    def gathered(f):
        own[f].wait()
        for step in range(1, n_shot):
            share(f, step).wait_recv()

    tiles = [(r, b * BLK) for b in range(NY // BLK) for r in range(ROWS)]

    gathered(QUA)
    gathered(BUO)
    for r, y in tiles:
        at = (r, slice(y, y + BLK), slice(None))
        damping = jnp.exp(-TIME_STEP * model[(QUA, *at)])
        model[(QUA, *at)] = damping - 1.0
        model[(BUO, *at)] = (TIME_STEP / 24.0) * damping * model[(BUO, *at)]

    wide = lax.broadcasted_iota(jnp.int32, (BLK, NZ), 1)

    def at(f, r, y, dy=0):
        return fields[f, LO + r, PAD + y + dy:PAD + y + dy + BLK, :]

    def near_far(back, back2, here, ahead, ahead2, forward):
        if forward:
            return ahead - here, ahead2 - back
        return here - back, ahead - back2

    def along_x(f, r, y, forward):
        if forward:
            return at(f, r + 1, y) - at(f, r, y), at(f, r + 2, y) - at(f, r - 1, y)
        return at(f, r, y) - at(f, r - 1, y), at(f, r + 1, y) - at(f, r - 2, y)

    def along_y(f, r, y, forward):
        if forward:
            return at(f, r, y, 1) - at(f, r, y), at(f, r, y, 2) - at(f, r, y, -1)
        return at(f, r, y) - at(f, r, y, -1), at(f, r, y, 1) - at(f, r, y, -2)

    def along_z(f, r, y, forward):
        here = at(f, r, y)

        def moved(k):
            turned = pltpu.roll(here, (-k) % NZ, 1)
            return jnp.where(wide < NZ - k if k > 0 else wide >= -k, turned, 0.0)

        if forward:
            return moved(1) - here, moved(2) - moved(-1)
        return here - moved(-1), moved(1) - moved(-2)

    def total(*parts):
        near = sum(p[0] for p in parts[1:]) + parts[0][0]
        far = sum(p[1] for p in parts[1:]) + parts[0][1]
        return 27.0 * near - far

    def mask_of(t, y):
        return jnp.tile(masks[t, y // BLK], (BLK // 8, 1))

    def keep(t, r, y, mask):
        return 1.0 + mask * model[QUA, r, y:y + BLK, :]

    def put(f, r, y, value):
        fields[f, LO + r, PAD + y:PAD + y + BLK, :] = value

    def velocity(t, f, gradient):
        for r, y in tiles:
            mask = mask_of(t, y)
            factor = mask * model[BUO, r, y:y + BLK, :]
            put(f, r, y, keep(t, r, y, mask) * at(f, r, y) + factor * gradient(r, y))

    def normal(t):
        for r, y in tiles:
            mask = mask_of(t, y)
            kept = keep(t, r, y, mask)
            shear = mask * model[MU, r, y:y + BLK, :]
            twice = shear + shear
            strain = [total(along_x(VX, r, y, False)), total(along_y(VY, r, y, False)), total(along_z(VZ, r, y, False))]
            swell = mask * model[LAM, r, y:y + BLK, :] * (strain[0] + strain[1] + strain[2])
            for f, part in zip((SXX, SYY, SZZ), strain):
                put(f, r, y, kept * at(f, r, y) + (swell + twice * part))

    def sheared(t, f, gradient):
        for r, y in tiles:
            mask = mask_of(t, y)
            factor = mask * model[MU, r, y:y + BLK, :]
            put(f, r, y, keep(t, r, y, mask) * at(f, r, y) + factor * gradient(r, y))

    for copy in loads:
        copy.wait()

    def body(t, carry):
        again = t < STEPS - 1

        def reuse(f):
            @pl.when(t > 0)
            def _():
                sent(f)

        arrived(SXX)
        reuse(VX)
        velocity(t, VX, lambda r, y: total(along_x(SXX, r, y, True), along_y(SXY, r, y, False), along_z(SXZ, r, y, False)))
        send(VX)
        arrived(SXY)
        reuse(VY)
        velocity(t, VY, lambda r, y: total(along_x(SXY, r, y, False), along_y(SYY, r, y, True), along_z(SYZ, r, y, False)))
        send(VY)
        arrived(SXZ)
        reuse(VZ)
        velocity(t, VZ, lambda r, y: total(along_x(SXZ, r, y, False), along_y(SYZ, r, y, False), along_z(SZZ, r, y, True)))
        send(VZ)

        @pl.when(t == 0)
        def _():
            gathered(LAM)
            gathered(MU)
            for r, y in tiles:
                spot = (r, slice(y, y + BLK), slice(None))
                factor = (TIME_STEP / 24.0) * (model[(QUA, *spot)] + 1.0)
                model[(LAM, *spot)] = factor * model[(LAM, *spot)]
                model[(MU, *spot)] = factor * model[(MU, *spot)]

        sheared(t, SYZ, lambda r, y: total(along_z(VY, r, y, True), along_y(VZ, r, y, True)))
        arrived(VX)
        sent(SXX)
        normal(t)

        @pl.when(again)
        def _():
            send(SXX)

        arrived(VY)
        sent(SXY)
        sheared(t, SXY, lambda r, y: total(along_y(VX, r, y, True), along_x(VY, r, y, True)))

        @pl.when(again)
        def _():
            send(SXY)

        arrived(VZ)
        sent(SXZ)
        sheared(t, SXZ, lambda r, y: total(along_z(VX, r, y, True), along_x(VZ, r, y, True)))

        @pl.when(again)
        def _():
            send(SXZ)

        return carry

    lax.fori_loop(0, STEPS, body, 0)

    stores = [pltpu.make_async_copy(inside(f, pl.ds(LO, ROWS)), out.at[f], out_sem.at[f]) for f in range(9)]
    for copy in stores:
        copy.start()
    for f in (VX, VY, VZ):
        sent(f)
    for f in range(4):
        for step in range(1, n_shot):
            share(f, step).wait_send()
    for copy in stores:
        copy.wait()


def solution(mesh):
    n_aper, n_shot = mesh.shape["aper"], mesh.shape["shot"]

    def per_device(wavefield, lame_lambda, lame_mu, buoyancy, quality, active):
        hbm = pl.BlockSpec(memory_space=pltpu.HBM)
        result = pl.pallas_call(
            functools.partial(kernel, n_aper, n_shot),
            out_shape=jax.ShapeDtypeStruct((9, ROWS, NY, NZ), jnp.float32),
            in_specs=[hbm] * 6,
            out_specs=pl.BlockSpec(memory_space=pl.ANY),
            scratch_shapes=[
                pltpu.VMEM((9, ROWS + 2 * LO, NY + 2 * PAD, NZ), jnp.float32),
                pltpu.VMEM((4, ROWS, NY, NZ), jnp.float32),
                pltpu.VMEM((STEPS, NY // BLK, 8, NZ), jnp.float32),
                pltpu.SMEM((STEPS, NY // BLK, NZ // BLK, n_aper), jnp.int32),
                pltpu.SemaphoreType.DMA((9,)),
                pltpu.SemaphoreType.DMA,
                pltpu.SemaphoreType.DMA((4,)),
                pltpu.SemaphoreType.DMA((4, n_shot - 1)),
                pltpu.SemaphoreType.DMA((4, n_shot - 1)),
                pltpu.SemaphoreType.DMA((9, 2)),
                pltpu.SemaphoreType.DMA((9, 2)),
                pltpu.SemaphoreType.DMA((9,)),
            ],
            compiler_params=pltpu.CompilerParams(
                collective_id=0, has_side_effects=True, vmem_limit_bytes=60 * 1024 * 1024
            ),
            name="elastic_steps",
        )(wavefield[0], lame_lambda, lame_mu, buoyancy, quality, jnp.transpose(active, (0, 2, 3, 1)))
        return result[None]

    return jax.shard_map(
        per_device,
        mesh=mesh,
        in_specs=(
            P("shot", None, "aper", None, None),
            P("aper", "shot", None),
            P("aper", "shot", None),
            P("aper", "shot", None),
            P("aper", "shot", None),
            P(),
        ),
        out_specs=P("shot", None, "aper", None, None),
        check_vma=False,
    )
```

time: 354 us -> 136 us (0.38)
  the two profiles are of different devices: /device:TPU:126 before, /device:TPU:94 now
where the time goes in v1:
time: 136 us
  Pallas kernels  133 us (98%)
  local copies, waits for them, and re-layouts  3.32 us (2%)
    pallas_call x1, Pallas kernels, per_device(): pl.pallas_call(functools.partial(kernel, n_aper, n_shot), out_shape=jax.S...  133 us
    unnamed x1, local copies, waits for them, and re-layouts  3.32 us

profile of v1, /device:TPU:94, one launch (start us, length us, event | category | flops | bytes accessed | tf_op | source)
XLA Modules:
  0.0 136.2 jit_solution(14953952903368291293)
XLA Ops:
  0.0 132.9 %elastic_steps.1 = f32[9,4,128,128]{3,2,1,0:T(8,128)} custom-call(f32[9,4,128,128]{3,2,1,0:T(8,128)} %bitcast.4, f32[4,32,128]{2,1,0:T(8,128)} %lam.1, f32[4,32,128]{2,1,0:T(8,128)} %mu.1, f32[4,32,128]{2,1,0:T(8,128)} %buo.1, f32[4,32,128]{2,1,0:T(8,128)} %qua.1, s32[4,4,4,64]{3,2,1,0:T(4,128)} %bitcast.5), custom_call_target="tpu_custom_call" | custom-call | tf_op jit(solution)/shard_map/elastic_steps/pallas_call | solution.py:304
  132.9 3.3 %copy.8 = f32[1,9,4,128,128]{4,3,2,1,0:T(8,128)} copy(f32[1,9,4,128,128]{4,3,2,1,0:T(8,128)} %bitcast.3) | data formatting | bytes 4718592

commit v2 on v1

v2 whole, which is shorter than its diff:
```python
import functools

import jax
import jax.numpy as jnp
from jax import lax
from jax.experimental import pallas as pl
from jax.experimental.pallas import tpu as pltpu
from jax.sharding import PartitionSpec as P

BLK = 32
STEPS = 4
TIME_STEP = 0.2
MESH = pl.DeviceIdType.MESH

VX, VY, VZ, SXX, SYY, SZZ, SXY, SXZ, SYZ = range(9)
LAM, MU, BUO, QUA = range(4)
ROWS = 4
NY = 128
NZ = 128
PAD = 8
LO = 2

PLANE = 16
SIDE = 4
PIECES = (64, 32, 32)

FORWARD = ((SXX, SXY), (SXZ,), (), (VX, VY), (VZ,), ())

LAYERS = {SXX: (1, 2), SXY: (2, 1), SXZ: (2, 1), VX: (2, 1), VY: (1, 2), VZ: (1, 2)}


def kernel(n_aper, n_shot, w, lam, mu, buo, qua, act, out, fields, model, masks, blocks, load_sem, act_sem, own_sem,
           gather_send, gather_recv, halo_send, halo_recv, out_sem, relay, leg_send, leg_recv, onward_send):
    me = lax.axis_index("aper")
    shot = lax.axis_index("shot")
    has_up = me < n_aper - 1
    has_down = me > 0
    up = jnp.minimum(me + 1, n_aper - 1)
    down = jnp.maximum(me - 1, 0)
    width = NY // n_shot
    shards = (lam, mu, buo, qua)

    def inside(f, rows):
        return fields.at[f, rows, PAD:PAD + NY, :]

    local = lax.rem(me, PLANE)
    last_plane = me >= n_aper - PLANE
    first_plane = me < PLANE
    crosses_up = jnp.logical_and(local == PLANE - 1, jnp.logical_not(last_plane))
    crosses_down = jnp.logical_and(local == 0, jnp.logical_not(first_plane))
    plain_up = jnp.logical_and(has_up, jnp.logical_not(crosses_up))
    plain_down = jnp.logical_and(has_down, jnp.logical_not(crosses_down))
    not_last, not_first = jnp.logical_not(last_plane), jnp.logical_not(first_plane)
    roles = [
        (jnp.logical_and(local == PLANE - SIDE, not_last), SIDE - 1, SIDE, True, 1),
        (jnp.logical_and(local == SIDE - 1, not_last), PLANE - SIDE, PLANE - SIDE + 1, True, 2),
        (jnp.logical_and(local == SIDE - 1, not_first), 1 - SIDE, -SIDE, False, 1),
        (jnp.logical_and(local == PLANE - SIDE, not_first), SIDE - PLANE, SIDE - PLANE - 1, False, 2),
    ]
    starts = [sum(PIECES[:k]) for k in range(len(PIECES))]

    def clipped(index):
        return jnp.clip(index, 0, n_aper - 1)

    def span(k):
        return pl.ds(PAD + starts[k], PIECES[k])

    def edge(f, to_up):
        count = LAYERS[f][0 if to_up else 1]
        if to_up:
            return pl.ds(LO + ROWS - count, count), pl.ds(LO - count, count)
        return pl.ds(LO, count), pl.ds(LO + ROWS, count)

    def leaving(f, to_up, ys, source):
        rows = edge(f, to_up)[0]
        if source is None:
            return fields.at[f, rows, ys, :]
        return source.at[f, pl.ds(rows.start - LO, rows.size), pl.ds(ys.start - PAD, ys.size), :]

    def halo(f, to_up, k=None, source=None):
        ys = pl.ds(PAD, NY) if k is None else span(k)
        side = 0 if to_up else 1
        return pltpu.make_async_remote_copy(
            src_ref=leaving(f, to_up, ys, source), dst_ref=fields.at[f, edge(f, to_up)[1], ys, :],
            send_sem=halo_send.at[f, side], recv_sem=halo_recv.at[f, side, k or 0],
            device_id=(up if to_up else down, shot), device_id_type=MESH)

    def leg(f, to_up, k, source=None, t=0):
        away = SIDE - 1 if k == 1 else PLANE - SIDE
        target = me - away if to_up else me + away
        return pltpu.make_async_remote_copy(
            src_ref=leaving(f, to_up, span(k), source),
            dst_ref=relay.at[t, 0 if to_up else 1, f, pl.ds(0, edge(f, to_up)[0].size), pl.ds(0, PIECES[k]), :],
            send_sem=leg_send.at[f, k - 1], recv_sem=leg_recv.at[f, 0 if to_up else 1], device_id=(clipped(target), shot), device_id_type=MESH)

    def onward(f, role, t=0):
        _, _, offset, to_up, k = role
        rows, side = edge(f, to_up)[1], 0 if to_up else 1
        return pltpu.make_async_remote_copy(
            src_ref=relay.at[t, side, f, pl.ds(0, rows.size), pl.ds(0, PIECES[k]), :], dst_ref=fields.at[f, rows, span(k), :],
            send_sem=onward_send.at[f, side], recv_sem=halo_recv.at[f, side, k],
            device_id=(clipped(me + offset), shot), device_id_type=MESH)

    def send(f, t, source=None):
        for to_up, crosses, plain in ((True, crosses_up, plain_up), (False, crosses_down, plain_down)):
            @pl.when(crosses)
            def _():
                leg(f, to_up, 1, source, t).start()
                leg(f, to_up, 2, source, t).start()
                halo(f, to_up, 0, source).start()

            @pl.when(plain)
            def _():
                halo(f, to_up, None, source).start()

    def sent(f):
        for to_up, crosses, plain in ((True, crosses_up, plain_up), (False, crosses_down, plain_down)):
            @pl.when(crosses)
            def _():
                leg(f, to_up, 1).wait_send()
                leg(f, to_up, 2).wait_send()
                halo(f, to_up, 0).wait_send()

            @pl.when(plain)
            def _():
                halo(f, to_up).wait_send()

    def arrived(f):
        for to_up, crosses, plain in ((True, crosses_down, plain_down), (False, crosses_up, plain_up)):
            @pl.when(crosses)
            def _():
                for k in range(len(PIECES)):
                    halo(f, to_up, k).wait_recv()

            @pl.when(plain)
            def _():
                halo(f, to_up).wait_recv()

    def forward(t, *some):
        for f in some:
            for role in roles:
                @pl.when(role[0])
                def _():
                    @pl.when(t > 0)
                    def _():
                        onward(f, role).wait_send()

                    leg(f, role[3], role[4]).wait_recv()
                    onward(f, role, t).start()

    partner = shot + 1 - 2 * lax.rem(shot, 2)
    across = lax.rem(shot + 2, n_shot)

    def shard_rows(owner):
        return pl.ds(pl.multiple_of(owner * width, width), width)

    def share(f, hop):
        place = model.at[f, :, shard_rows(across if hop == 2 else shot), :]
        return pltpu.make_async_remote_copy(
            src_ref=place if hop == 2 else shards[f], dst_ref=place, send_sem=gather_send.at[f, hop],
            recv_sem=gather_recv.at[f, hop], device_id=(me, across if hop == 1 else partner), device_id_type=MESH)

    def pass_on(f):
        share(f, 1).wait_recv()
        share(f, 2).start()

    loads = [pltpu.make_async_copy(w.at[f], inside(f, pl.ds(LO, ROWS)), load_sem.at[f]) for f in range(9)]
    own = [pltpu.make_async_copy(shards[f], model.at[f, :, shard_rows(shot), :], own_sem.at[f]) for f in range(4)]
    flags = pltpu.make_async_copy(act, blocks, act_sem)

    barrier = pltpu.get_barrier_semaphore()

    greeted = [(has_up, me + 1), (has_down, me - 1)]
    for crossing, sign in ((crosses_up, 1), (crosses_down, -1)):
        greeted += [(crossing, me - sign * (SIDE - 1)), (crossing, me - sign * (PLANE - SIDE)),
                    (crossing, me + sign * SIDE), (crossing, me + sign * (PLANE - SIDE + 1))]
    for here, origin, target, _, _ in roles:
        greeted += [(here, me + origin), (here, me + target)]
    for here, whom in greeted:
        @pl.when(here)
        def _():
            pl.semaphore_signal(barrier, inc=1, device_id=(clipped(whom), shot), device_id_type=MESH)

    for peer in (partner, across):
        pl.semaphore_signal(barrier, inc=1, device_id=(me, peer), device_id_type=MESH)

    flags.start()
    for copy in loads + own:
        copy.start()

    zeros = jnp.zeros((ROWS, PAD, NZ), jnp.float32)
    for f in range(9):
        fields[f, LO:LO + ROWS, 0:PAD, :] = zeros
        fields[f, LO:LO + ROWS, PAD + NY:, :] = zeros

    @pl.when(jnp.logical_not(has_down))
    def _():
        for f in LAYERS:
            fields[f, 0:LO, PAD:PAD + NY, :] = jnp.zeros((LO, NY, NZ), jnp.float32)

    @pl.when(jnp.logical_not(has_up))
    def _():
        for f in LAYERS:
            fields[f, LO + ROWS:, PAD:PAD + NY, :] = jnp.zeros((LO, NY, NZ), jnp.float32)

    pl.semaphore_wait(barrier, 2 + sum(here.astype(jnp.int32) for here, _ in greeted))

    for f in (QUA, BUO):
        for hop in (1, 0):
            share(f, hop).start()
    for f in (SXX, SXY, SXZ):
        send(f, 0, w)
    for f in (LAM, MU):
        for hop in (1, 0):
            share(f, hop).start()

    lane = lax.broadcasted_iota(jnp.int32, (8, NZ), 1)
    flags.wait()
    for t in range(STEPS):
        for b in range(NY // BLK):
            on = [blocks[t, b, k, me].astype(jnp.float32) for k in range(NZ // BLK)]
            masks[t, b] = jnp.where(lane < BLK, on[0], jnp.where(lane < 2 * BLK, on[1],
                                    jnp.where(lane < 3 * BLK, on[2], on[3])))

    def gathered(f):
        own[f].wait()
        for hop in (0, 2):
            share(f, hop).wait_recv()
        share(f, 2).wait_send()

    tiles = [(r, b * BLK) for b in range(NY // BLK) for r in range(ROWS)]

    pass_on(QUA)
    pass_on(BUO)
    gathered(QUA)
    gathered(BUO)
    for r, y in tiles:
        at = (r, slice(y, y + BLK), slice(None))
        damping = jnp.exp(-TIME_STEP * model[(QUA, *at)])
        model[(QUA, *at)] = damping - 1.0
        model[(BUO, *at)] = (TIME_STEP / 24.0) * damping * model[(BUO, *at)]

    wide = lax.broadcasted_iota(jnp.int32, (BLK, NZ), 1)

    def at(f, r, y, dy=0):
        return fields[f, LO + r, PAD + y + dy:PAD + y + dy + BLK, :]

    def along_x(f, r, y, forward):
        if forward:
            return at(f, r + 1, y) - at(f, r, y), at(f, r + 2, y) - at(f, r - 1, y)
        return at(f, r, y) - at(f, r - 1, y), at(f, r + 1, y) - at(f, r - 2, y)

    def along_y(f, r, y, forward):
        if forward:
            return at(f, r, y, 1) - at(f, r, y), at(f, r, y, 2) - at(f, r, y, -1)
        return at(f, r, y) - at(f, r, y, -1), at(f, r, y, 1) - at(f, r, y, -2)

    def along_z(f, r, y, forward):
        here = at(f, r, y)

        def moved(k):
            turned = pltpu.roll(here, (-k) % NZ, 1)
            return jnp.where(wide < NZ - k if k > 0 else wide >= -k, turned, 0.0)

        if forward:
            return moved(1) - here, moved(2) - moved(-1)
        return here - moved(-1), moved(1) - moved(-2)

    def total(*parts):
        near, far = parts[0]
        for more in parts[1:]:
            near, far = near + more[0], far + more[1]
        return 27.0 * near - far

    def mask_of(t, y):
        return jnp.tile(masks[t, y // BLK], (BLK // 8, 1))

    def keep(t, r, y, mask):
        return 1.0 + mask * model[QUA, r, y:y + BLK, :]

    def put(f, r, y, value):
        fields[f, LO + r, PAD + y:PAD + y + BLK, :] = value

    def begin(t, f, coefficient, gradient):
        for r, y in tiles:
            mask = mask_of(t, y)
            factor = mask * model[coefficient, r, y:y + BLK, :]
            put(f, r, y, keep(t, r, y, mask) * at(f, r, y) + factor * gradient(r, y))

    def finish(t, f, coefficient, gradient):
        for r, y in tiles:
            factor = mask_of(t, y) * model[coefficient, r, y:y + BLK, :]
            put(f, r, y, at(f, r, y) + factor * gradient(r, y))

    def begin_normal(t):
        for r, y in tiles:
            mask = mask_of(t, y)
            kept = keep(t, r, y, mask)
            shear = mask * model[MU, r, y:y + BLK, :]
            twice = shear + shear
            second, third = total(along_y(VY, r, y, False)), total(along_z(VZ, r, y, False))
            swell = mask * model[LAM, r, y:y + BLK, :] * (second + third)
            put(SXX, r, y, kept * at(SXX, r, y) + swell)
            put(SYY, r, y, kept * at(SYY, r, y) + (swell + twice * second))
            put(SZZ, r, y, kept * at(SZZ, r, y) + (swell + twice * third))

    def finish_normal(t):
        for r, y in tiles:
            mask = mask_of(t, y)
            first = mask * total(along_x(VX, r, y, False))
            shear = model[MU, r, y:y + BLK, :]
            swell = model[LAM, r, y:y + BLK, :] * first
            put(SXX, r, y, at(SXX, r, y) + (swell + (shear + shear) * first))
            put(SYY, r, y, at(SYY, r, y) + swell)
            put(SZZ, r, y, at(SZZ, r, y) + swell)

    for copy in loads:
        copy.wait()

    def body(t, carry):
        again = t < STEPS - 1

        def reuse(f):
            @pl.when(t > 0)
            def _():
                sent(f)

        reuse(VX)
        begin(t, VX, BUO, lambda r, y: total(along_y(SXY, r, y, False), along_z(SXZ, r, y, False)))
        reuse(VY)
        begin(t, VY, BUO, lambda r, y: total(along_y(SYY, r, y, True), along_z(SYZ, r, y, False)))
        reuse(VZ)
        begin(t, VZ, BUO, lambda r, y: total(along_y(SYZ, r, y, False), along_z(SZZ, r, y, True)))
        forward(t, *FORWARD[0])
        arrived(SXX)
        finish(t, VX, BUO, lambda r, y: total(along_x(SXX, r, y, True)))
        send(VX, t)
        forward(t, *FORWARD[1])
        arrived(SXY)
        finish(t, VY, BUO, lambda r, y: total(along_x(SXY, r, y, False)))
        send(VY, t)

        @pl.when(t == 0)
        def _():
            pass_on(LAM)
            pass_on(MU)

        forward(t, *FORWARD[2])
        arrived(SXZ)
        finish(t, VZ, BUO, lambda r, y: total(along_x(SXZ, r, y, False)))
        send(VZ, t)

        @pl.when(t == 0)
        def _():
            gathered(LAM)
            gathered(MU)
            for r, y in tiles:
                spot = (r, slice(y, y + BLK), slice(None))
                factor = (TIME_STEP / 24.0) * (model[(QUA, *spot)] + 1.0)
                model[(LAM, *spot)] = factor * model[(LAM, *spot)]
                model[(MU, *spot)] = factor * model[(MU, *spot)]

        sent(SXX)
        begin_normal(t)
        sent(SXY)
        begin(t, SXY, MU, lambda r, y: total(along_y(VX, r, y, True)))
        sent(SXZ)
        begin(t, SXZ, MU, lambda r, y: total(along_z(VX, r, y, True)))
        begin(t, SYZ, MU, lambda r, y: total(along_z(VY, r, y, True), along_y(VZ, r, y, True)))
        forward(t, *FORWARD[3])
        arrived(VX)
        finish_normal(t)

        @pl.when(again)
        def _():
            send(SXX, t + 1)

        forward(t, *FORWARD[4])
        arrived(VY)
        finish(t, SXY, MU, lambda r, y: total(along_x(VY, r, y, True)))

        @pl.when(again)
        def _():
            send(SXY, t + 1)

        forward(t, *FORWARD[5])
        arrived(VZ)
        finish(t, SXZ, MU, lambda r, y: total(along_x(VZ, r, y, True)))

        @pl.when(again)
        def _():
            send(SXZ, t + 1)

        return carry

    lax.fori_loop(0, STEPS, body, 0)

    stores = [pltpu.make_async_copy(inside(f, pl.ds(LO, ROWS)), out.at[f], out_sem.at[f]) for f in range(9)]
    for copy in stores:
        copy.start()
    for f in (VX, VY, VZ):
        sent(f)
    for role in roles:
        @pl.when(role[0])
        def _():
            for f in LAYERS:
                onward(f, role).wait_send()

    for f in range(4):
        for hop in range(2):
            share(f, hop).wait_send()
    for copy in stores:
        copy.wait()


def solution(mesh):
    n_aper, n_shot = mesh.shape["aper"], mesh.shape["shot"]

    def per_device(wavefield, lame_lambda, lame_mu, buoyancy, quality, active):
        hbm = pl.BlockSpec(memory_space=pltpu.HBM)
        result = pl.pallas_call(
            functools.partial(kernel, n_aper, n_shot),
            out_shape=jax.ShapeDtypeStruct((9, ROWS, NY, NZ), jnp.float32),
            in_specs=[hbm] * 6,
            out_specs=pl.BlockSpec(memory_space=pl.ANY),
            scratch_shapes=[
                pltpu.VMEM((9, ROWS + 2 * LO, NY + 2 * PAD, NZ), jnp.float32),
                pltpu.VMEM((4, ROWS, NY, NZ), jnp.float32),
                pltpu.VMEM((STEPS, NY // BLK, 8, NZ), jnp.float32),
                pltpu.SMEM((STEPS, NY // BLK, NZ // BLK, n_aper), jnp.int32),
                pltpu.SemaphoreType.DMA((9,)),
                pltpu.SemaphoreType.DMA,
                pltpu.SemaphoreType.DMA((4,)),
                pltpu.SemaphoreType.DMA((4, 3)),
                pltpu.SemaphoreType.DMA((4, 3)),
                pltpu.SemaphoreType.DMA((9, 2)),
                pltpu.SemaphoreType.DMA((9, 2, 3)),
                pltpu.SemaphoreType.DMA((9,)),
                pltpu.VMEM((STEPS, 2, 9, LO, max(PIECES[1:]), NZ), jnp.float32),
                pltpu.SemaphoreType.DMA((9, 2)),
                pltpu.SemaphoreType.DMA((9, 2)),
                pltpu.SemaphoreType.DMA((9, 2)),
            ],
            compiler_params=pltpu.CompilerParams(
                collective_id=0, has_side_effects=True, vmem_limit_bytes=60 * 1024 * 1024
            ),
            name="elastic_steps",
        )(wavefield[0], lame_lambda, lame_mu, buoyancy, quality, jnp.transpose(active, (0, 2, 3, 1)))
        return result[None]

    return jax.shard_map(
        per_device,
        mesh=mesh,
        in_specs=(
            P("shot", None, "aper", None, None),
            P("aper", "shot", None),
            P("aper", "shot", None),
            P("aper", "shot", None),
            P("aper", "shot", None),
            P(),
        ),
        out_specs=P("shot", None, "aper", None, None),
        check_vma=False,
    )
```

time: 136 us -> 94.2 us (0.69)
  Pallas kernels: 133 us -> 89.9 us
    pallas_call x1, Pallas kernels: 133 us -> 89.9 us  [per_device(): pl.pallas_call(functools.partial(kernel, n_aper, n_shot), out_shape=jax.S...]
where the time goes in v2:
time: 94.2 us; the launch traced here: 93.2 us
  Pallas kernels  89.9 us (95%)
  local copies, waits for them, and re-layouts  3.32 us (4%)
    pallas_call x1, Pallas kernels, per_device(): pl.pallas_call(functools.partial(kernel, n_aper, n_shot), out_shape=jax.S...  89.9 us
    unnamed x1, local copies, waits for them, and re-layouts  3.32 us

profile of v2, /device:TPU:94, one launch (start us, length us, event | category | flops | bytes accessed | tf_op | source)
XLA Modules:
  0.0 93.2 jit_solution(11474122434344362852)
XLA Ops:
  0.0 89.9 %elastic_steps.1 = f32[9,4,128,128]{3,2,1,0:T(8,128)} custom-call(f32[9,4,128,128]{3,2,1,0:T(8,128)} %bitcast.4, f32[4,32,128]{2,1,0:T(8,128)} %lam.1, f32[4,32,128]{2,1,0:T(8,128)} %mu.1, f32[4,32,128]{2,1,0:T(8,128)} %buo.1, f32[4,32,128]{2,1,0:T(8,128)} %qua.1, s32[4,4,4,64]{3,2,1,0:T(4,128)} %bitcast.5), custom_call_target="tpu_custom_call" | custom-call | tf_op jit(solution)/shard_map/elastic_steps/pallas_call | solution.py:421
  89.9 3.3 %copy.8 = f32[1,9,4,128,128]{4,3,2,1,0:T(8,128)} copy(f32[1,9,4,128,128]{4,3,2,1,0:T(8,128)} %bitcast.3) | data formatting | bytes 4718592

commit v3 on v2

--- a/solution.py
+++ b/solution.py
@@ -22,8 +22,9 @@
 
 PLANE = 16
 SIDE = 4
-PIECES = (64, 32, 32)
-
+PIECES = (56, 32, 40)
+
+FIRST = 0
 FORWARD = ((SXX, SXY), (SXZ,), (), (VX, VY), (VZ,), ())
 
 LAYERS = {SXX: (1, 2), SXY: (2, 1), SXZ: (2, 1), VX: (2, 1), VY: (1, 2), VZ: (1, 2)}
@@ -136,17 +137,28 @@
             def _():
                 halo(f, to_up).wait_recv()
 
-    def forward(t, *some):
+    def relayed(t, *some):
         for f in some:
             for role in roles:
                 @pl.when(role[0])
                 def _():
-                    @pl.when(t > 0)
-                    def _():
-                        onward(f, role).wait_send()
+                    if t is not FIRST:
+                        @pl.when(t > 0)
+                        def _():
+                            onward(f, role).wait_send()
 
                     leg(f, role[3], role[4]).wait_recv()
                     onward(f, role, t).start()
+
+    def forward(t, *some):
+        now = [f for f in some if f in (VX, VY, VZ)]
+        if now:
+            relayed(t, *now)
+        later = [f for f in some if f not in now]
+        if later:
+            @pl.when(t > 0)
+            def _():
+                relayed(t, *later)
 
     partner = shot + 1 - 2 * lax.rem(shot, 2)
     across = lax.rem(shot + 2, n_shot)
@@ -221,6 +233,8 @@
             on = [blocks[t, b, k, me].astype(jnp.float32) for k in range(NZ // BLK)]
             masks[t, b] = jnp.where(lane < BLK, on[0], jnp.where(lane < 2 * BLK, on[1],
                                     jnp.where(lane < 3 * BLK, on[2], on[3])))
+
+    relayed(FIRST, SXX, SXY, SXZ)
 
     def gathered(f):
         own[f].wait()
@@ -317,8 +331,16 @@
     for copy in loads:
         copy.wait()
 
+    stores = [pltpu.make_async_copy(inside(f, pl.ds(LO, ROWS)), out.at[f], out_sem.at[f]) for f in range(9)]
+
     def body(t, carry):
         again = t < STEPS - 1
+
+        def store(*some):
+            @pl.when(t == STEPS - 1)
+            def _():
+                for f in some:
+                    stores[f].start()
 
         def reuse(f):
             @pl.when(t > 0)
@@ -335,23 +357,23 @@
         arrived(SXX)
         finish(t, VX, BUO, lambda r, y: total(along_x(SXX, r, y, True)))
         send(VX, t)
+        store(VX)
         forward(t, *FORWARD[1])
         arrived(SXY)
         finish(t, VY, BUO, lambda r, y: total(along_x(SXY, r, y, False)))
         send(VY, t)
-
-        @pl.when(t == 0)
-        def _():
-            pass_on(LAM)
-            pass_on(MU)
+        store(VY)
 
         forward(t, *FORWARD[2])
         arrived(SXZ)
         finish(t, VZ, BUO, lambda r, y: total(along_x(SXZ, r, y, False)))
         send(VZ, t)
+        store(VZ)
 
         @pl.when(t == 0)
         def _():
+            pass_on(LAM)
+            pass_on(MU)
             gathered(LAM)
             gathered(MU)
             for r, y in tiles:
@@ -375,6 +397,8 @@
         def _():
             send(SXX, t + 1)
 
+        store(SXX, SYY, SZZ, SYZ)
+
         forward(t, *FORWARD[4])
         arrived(VY)
         finish(t, SXY, MU, lambda r, y: total(along_x(VY, r, y, True)))
@@ -383,6 +407,8 @@
         def _():
             send(SXY, t + 1)
 
+        store(SXY)
+
         forward(t, *FORWARD[5])
         arrived(VZ)
         finish(t, SXZ, MU, lambda r, y: total(along_x(VZ, r, y, True)))
@@ -391,13 +417,12 @@
         def _():
             send(SXZ, t + 1)
 
+        store(SXZ)
+
         return carry
 
     lax.fori_loop(0, STEPS, body, 0)
 
-    stores = [pltpu.make_async_copy(inside(f, pl.ds(LO, ROWS)), out.at[f], out_sem.at[f]) for f in range(9)]
-    for copy in stores:
-        copy.start()
     for f in (VX, VY, VZ):
         sent(f)
     for role in roles:
@@ -442,10 +467,10 @@
                 pltpu.SemaphoreType.DMA((9, 2)),
             ],
             compiler_params=pltpu.CompilerParams(
-                collective_id=0, has_side_effects=True, vmem_limit_bytes=60 * 1024 * 1024
+                collective_id=0, has_side_effects=True, vmem_limit_bytes=32 * 2**20
             ),
             name="elastic_steps",
-        )(wavefield[0], lame_lambda, lame_mu, buoyancy, quality, jnp.transpose(active, (0, 2, 3, 1)))
+        )(*(pltpu.with_memory_space_constraint(x, pltpu.HBM) for x in (wavefield[0], lame_lambda, lame_mu, buoyancy, quality, jnp.transpose(active, (0, 2, 3, 1)))))
         return result[None]
 
     return jax.shard_map(

time: 94.2 us -> 88.6 us (0.941)
  Pallas kernels: 89.9 us -> 86.7 us
  local copies, waits for them, and re-layouts: 3.32 us -> 1.41 us
    pallas_call x1, Pallas kernels: 89.9 us -> 86.7 us  [per_device(): pl.pallas_call(functools.partial(kernel, n_aper, n_shot), out_shape=jax.S...]
    unnamed x1, local copies, waits for them, and re-layouts: 3.32 us -> 1.41 us
where the time goes in v3:
time: 88.6 us; the launch traced here: 88.1 us
  Pallas kernels  86.7 us (98%)
  local copies, waits for them, and re-layouts  1.41 us (2%)
    pallas_call x1, Pallas kernels, per_device(): pl.pallas_call(functools.partial(kernel, n_aper, n_shot), out_shape=jax.S...  86.7 us

profile of v3, /device:TPU:94, one launch (start us, length us, event | category | flops | bytes accessed | tf_op | source)
XLA Modules:
  0.0 88.1 jit_solution(18079499772611929822)
XLA Ops:
  0.0 86.7 %elastic_steps.1 = f32[9,4,128,128]{3,2,1,0:T(8,128)S(1)} custom-call(f32[9,4,128,128]{3,2,1,0:T(8,128)} %bitcast.4, f32[4,32,128]{2,1,0:T(8,128)} %lam.1, f32[4,32,128]{2,1,0:T(8,128)} %mu.1, f32[4,32,128]{2,1,0:T(8,128)} %buo.1, f32[4,32,128]{2,1,0:T(8,128)} %qua.1, s32[4,4,4,64]{3,2,1,0:T(4,128)} %bitcast.5), custom_call_target="tpu_custom_call" | custom-call | tf_op jit(solution)/shard_map/elastic_steps/pallas_call | solution.py:446
  86.7 1.4 %copy.8 = f32[1,9,4,128,128]{4,3,2,1,0:T(8,128)} copy(f32[1,9,4,128,128]{4,3,2,1,0:T(8,128)S(1)} %bitcast.3) | data formatting | bytes 4718592

commit v4 on v3

--- a/solution.py
+++ b/solution.py
@@ -25,7 +25,7 @@
 PIECES = (56, 32, 40)
 
 FIRST = 0
-FORWARD = ((SXX, SXY), (SXZ,), (), (VX, VY), (VZ,), ())
+FORWARD = ((SXX,), (SXY,), (SXZ,), (VX,), (VY,), (VZ,))
 
 LAYERS = {SXX: (1, 2), SXY: (2, 1), SXZ: (2, 1), VX: (2, 1), VY: (1, 2), VZ: (1, 2)}
 
@@ -222,9 +222,6 @@
             share(f, hop).start()
     for f in (SXX, SXY, SXZ):
         send(f, 0, w)
-    for f in (LAM, MU):
-        for hop in (1, 0):
-            share(f, hop).start()
 
     lane = lax.broadcasted_iota(jnp.int32, (8, NZ), 1)
     flags.wait()
@@ -248,6 +245,9 @@
     pass_on(BUO)
     gathered(QUA)
     gathered(BUO)
+    for f in (LAM, MU):
+        for hop in (1, 0):
+            share(f, hop).start()
     for r, y in tiles:
         at = (r, slice(y, y + BLK), slice(None))
         damping = jnp.exp(-TIME_STEP * model[(QUA, *at)])

time: 88.6 us -> 87.6 us (0.989)
  Pallas kernels: 86.7 us -> 85.3 us
    pallas_call x1, Pallas kernels: 86.7 us -> 85.3 us  [per_device(): pl.pallas_call(functools.partial(kernel, n_aper, n_shot), out_shape=jax.S...]
where the time goes in v4:
time: 87.6 us; the launch traced here: 86.8 us
  Pallas kernels  85.3 us (97%)
  local copies, waits for them, and re-layouts  1.41 us (2%)
    pallas_call x1, Pallas kernels, per_device(): pl.pallas_call(functools.partial(kernel, n_aper, n_shot), out_shape=jax.S...  85.3 us

profile of v4, /device:TPU:94, one launch (start us, length us, event | category | flops | bytes accessed | tf_op | source)
XLA Modules:
  0.0 86.8 jit_solution(2510789724833775106)
XLA Ops:
  0.0 85.3 %elastic_steps.1 = f32[9,4,128,128]{3,2,1,0:T(8,128)S(1)} custom-call(f32[9,4,128,128]{3,2,1,0:T(8,128)} %bitcast.4, f32[4,32,128]{2,1,0:T(8,128)} %lam.1, f32[4,32,128]{2,1,0:T(8,128)} %mu.1, f32[4,32,128]{2,1,0:T(8,128)} %buo.1, f32[4,32,128]{2,1,0:T(8,128)} %qua.1, s32[4,4,4,64]{3,2,1,0:T(4,128)} %bitcast.5), custom_call_target="tpu_custom_call" | custom-call | tf_op jit(solution)/shard_map/elastic_steps/pallas_call | solution.py:446
  85.3 1.4 %copy.8 = f32[1,9,4,128,128]{4,3,2,1,0:T(8,128)} copy(f32[1,9,4,128,128]{4,3,2,1,0:T(8,128)S(1)} %bitcast.3) | data formatting | bytes 4718592
